TPU v7x, 32 devices: a whole 2x2x4 slice. The times are simulated.
32 devices in a mesh: ia: 4 (over z), ja: 4 (over y, core), ka: 2 (over x).
Axes of the slice: x: 2, y: 2, z: 4, core: 2. Of those that a mesh axis runs over, the one named last changes fastest.
Arguments:
- tensor: float32 [8192, 8, 1024], P('ja', 'ka', 'ia'), may hold values from -6 to 6
- factor_a: float32 [1024, 128], P('ia'), may hold values from -1 to 1
- factor_c: float32 [8, 128], P('ka'), may hold values from -2 to 2
- gram_c: float32 [128, 128], replicated, may hold values from -12 to 24, as said below
Outputs:
- factor_b: float32 [8192, 128], P('ja')
- factor_c_new: float32 [8, 128], P('ka')
Inputs may be any that keep to these rules, and one draw needn't show every extreme that they name: `gram_c`: symmetric positive definite.
All inputs are finite; a program needn't handle non-finite values.
Results may differ from a plain program's by a relative error of at most 0.000071.
Values sent between devices are 32-bit elements; how exact they have to be, the bound alone decides.
A program may use at most 64 MiB of HBM per device.

v0:
```python
import jax
import jax.numpy as jnp
from jax import lax
from jax.sharding import PartitionSpec as P


def right_solve(rhs, system):
    lower = jnp.linalg.cholesky(system)
    middle = lax.linalg.triangular_solve(lower, rhs, left_side=False, lower=True, transpose_a=True)
    return lax.linalg.triangular_solve(
        lower, middle, left_side=False, lower=True, transpose_a=False
    )


def body(tensor, factor_a, factor_c, gram_c):
    high = lax.Precision.HIGHEST
    mode_two, mode_three, mode_one = tensor.shape
    rank = factor_a.shape[1]
    gram_a = lax.psum(
        jnp.dot(factor_a.T, factor_a, precision=high, preferred_element_type=jnp.float32), "ia"
    )
    system_b = gram_a * gram_c
    flat = jnp.dot(
        tensor.reshape(mode_two * mode_three, mode_one),
        factor_a,
        precision=high,
        preferred_element_type=jnp.float32,
    )
    partial_value = flat.reshape(mode_two, mode_three, rank)
    mttkrp_b = lax.psum(jnp.sum(partial_value * factor_c[None, :, :], axis=1), ("ia", "ka"))
    factor_b = right_solve(mttkrp_b, system_b)
    mttkrp_c = lax.psum(jnp.sum(partial_value * factor_b[:, None, :], axis=0), ("ia", "ja"))
    gram_b = lax.psum(
        jnp.dot(factor_b.T, factor_b, precision=high, preferred_element_type=jnp.float32), "ja"
    )
    factor_c_new = right_solve(mttkrp_c, gram_a * gram_b)
    return (factor_b, factor_c_new)


def solution(mesh):
    placed = (P("ja", "ka", "ia"), P("ia", None), P("ka", None), P())
    return jax.shard_map(
        body, mesh=mesh, in_specs=placed, out_specs=(P("ja", None), P("ka", None)), check_vma=False
    )
```

profile of v0, /device:TPU:0, one launch (start us, length us, event | category | flops | bytes accessed | tf_op | source)
XLA Modules:
  0.0 200.3 jit_solution(17277993881042223334)
XLA Ops:
  7.2 0.0 copy-start
  7.2 0.0 all-reduce.6.cloned.1.call-start
  7.2 0.8 copy-done
  8.1 1.0 fusion.15
  9.1 0.0 all-reduce.6.cloned.1.call-update
  9.1 0.0 copy-start.3
  9.1 0.0 all-reduce.4.cloned.1.call-start
  9.2 12.6 %multiply_reduce_fusion.1 = (f32[2048,128]{1,0:T(8,128)}, f32[2048,4,128]{2,0,1:T(8,128)}) fusion(f32[4,128]{1,0:T(4,128)} %param.7, f32[256,128]{1,0:T(8,128)S(1)} %copy-done, f32[2048,4,256]{2,1,0:T(4,128)} %param.5), kind=kOutput, calls=%fused_computation.3 | convolution fusion | flops 3223060480 | bytes 13764608 | tf_op jit(solution)/shard_map/dot_general | solution.py:23
  21.8 0.0 all-reduce.4.cloned.1.call-update
  21.8 0.2 all-reduce.8.cloned.1.call-start
  22.0 0.0 copy-done.3
  22.0 0.1 copy.8
  22.1 25.2 %all-reduce.6.cloned.1.call-done = f32[128,128]{0,1:T(8,128)} async-done(((f32[128,128]{0,1:T(8,128)}), f32[128,128]{0,1:T(8,128)}) %all-reduce.6.cloned.1.call-update) | async-done | bytes 65552 | tf_op jit(solution)/shard_map/psum | solution.py:19
  47.3 0.8 mul.24
  48.2 0.1 copy.9
  48.3 11.7 %cholesky.44 = f32[128,128]{1,0:T(8,128)S(1)} custom-call(f32[128,128]{1,0:T(8,128)S(1)} %fusion.14), custom_call_target="Cholesky" | custom-call | tf_op jit(solution)/shard_map/jit(cholesky)/cholesky | solution.py:8
  60.1 0.6 compare_reduce_fusion.1
  60.7 0.7 fusion.3
  61.4 9.8 %custom-call.12 = f32[1,128,128]{1,2,0:T(8,128)S(1)} custom-call(f32[1,128,128]{2,1,0:T(8,128)S(1)} %fusion.3), custom_call_target="InvertDiagBlocksLowerTriangular" | custom-call | tf_op jit(solution)/shard_map/triangular_solve | solution.py:9
  71.2 58.4 %all-reduce.4.cloned.1.call-done = f32[2048,128]{1,0:T(8,128)} async-done(((f32[2048,128]{1,0:T(8,128)}), f32[2048,128]{1,0:T(8,128)}) %all-reduce.4.cloned.1.call-update) | async-done | bytes 1048592 | tf_op jit(solution)/shard_map/psum | solution.py:30
  129.6 2.2 %fusion.12 = f32[2048,128]{1,0:T(8,128)S(1)} fusion(f32[2048,128]{1,0:T(8,128)} %all-reduce.4.cloned.1.call-done, f32[1,128,128]{1,2,0:T(8,128)S(1)} %custom-call.12), kind=kOutput, calls=%fused_computation.17 | convolution fusion | flops 402653184 | bytes 2162688 | tf_op jit(solution)/shard_map/triangular_solve | solution.py:9
  131.8 1.0 fusion.10
  132.8 0.0 copy-start.1
  132.8 0.0 copy-start.2
  132.8 2.4 %fusion.16 = f32[128,128]{0,1:T(8,128)} fusion(f32[2048,128]{1,0:T(8,128)S(1)} %fusion.10), kind=kOutput, calls=%fused_computation.28 | convolution fusion | flops 402653184 | bytes 1114112 | tf_op jit(solution)/shard_map/dot_general | solution.py:34
  135.2 0.0 all-reduce.8.cloned.1.call-update
  135.2 2.5 %multiply_reduce_fusion = f32[4,128]{1,0:T(4,128)S(1)} fusion(f32[2048,4,128]{2,0,1:T(8,128)} %get-tuple-element.4, f32[2048,128]{1,0:T(8,128)S(1)} %fusion.10), kind=kLoop, calls=%fused_computation.2 | loop fusion | flops 2096640 | bytes 5244928 | tf_op jit(solution)/shard_map/reduce_sum | solution.py:32
  137.7 31.2 %psum.30 = f32[4,128]{1,0:T(4,128)S(1)} all-reduce(f32[4,128]{1,0:T(4,128)S(1)} %multiply_reduce_fusion), channel_id=1, replica_groups=mesh['ia'=4,'ja'=4,'ka'=2] {'ia','ja'}, use_global_device_ids=true, to_apply=%region_6.8 | all-reduce | flops 512 | bytes 4096 | tf_op jit(solution)/shard_map/psum | solution.py:32
  169.0 0.0 all-reduce.8.cloned.1.call-done
  169.0 0.0 copy-done.2
  169.0 0.8 mul.27
  169.8 0.1 copy.11
  169.9 11.7 %cholesky.55 = f32[128,128]{1,0:T(8,128)S(1)} custom-call(f32[128,128]{1,0:T(8,128)S(1)} %fusion.9), custom_call_target="Cholesky" | custom-call | tf_op jit(solution)/shard_map/jit(cholesky)/cholesky | solution.py:8
  181.7 0.6 compare_reduce_fusion
  182.3 0.7 fusion.4
  183.0 9.8 %custom-call.13 = f32[1,128,128]{1,2,0:T(8,128)S(1)} custom-call(f32[1,128,128]{2,1,0:T(8,128)S(1)} %fusion.4), custom_call_target="InvertDiagBlocksLowerTriangular" | custom-call | tf_op jit(solution)/shard_map/triangular_solve | solution.py:9
  192.8 0.2 fusion.7
  193.0 0.8 fusion.5
  193.8 0.0 copy-done.1
  (4 shorter events, 0.1 us)
Async XLA Ops:
  7.2 0.9 copy-start
  7.2 40.2 %all-reduce.6.cloned.1.call-start = ((), (), s32[]{:S(2)}) async-start(), calls=%async_computation.1 | async-start | bytes 131072 | tf_op jit(solution)/shard_map/psum | solution.py:19
  9.1 12.9 %copy-start.3 = (f32[128,128]{1,0:T(8,128)S(1)}, f32[128,128]{1,0:T(8,128)}, u32[]{:S(2)}) copy-start(f32[128,128]{1,0:T(8,128)} %param.8) | copy-start | bytes 196612
  9.1 120.5 %all-reduce.4.cloned.1.call-start = ((), (), s32[]{:S(2)}) async-start(), calls=%async_computation | async-start | bytes 2097152 | tf_op jit(solution)/shard_map/psum | solution.py:30
  21.8 147.2 %all-reduce.8.cloned.1.call-start = ((), (), s32[]{:S(2)}) async-start(), calls=%async_computation.2 | async-start | bytes 131072 | tf_op jit(solution)/shard_map/psum | solution.py:33
  132.8 61.0 %copy-start.1 = (f32[2048,128]{1,0:T(8,128)}, f32[2048,128]{1,0:T(8,128)S(1)}, u32[]{:S(2)}) copy-start(f32[2048,128]{1,0:T(8,128)S(1)} %fusion.10) | copy-start | bytes 3145732
  132.8 36.2 %copy-start.2 = (f32[128,128]{0,1:T(8,128)S(1)}, f32[128,128]{0,1:T(8,128)}, u32[]{:S(2)}) copy-start(f32[128,128]{0,1:T(8,128)} %all-reduce.6.cloned.1.call-done) | copy-start | bytes 196612
Sparse Core Ops, SparseCore 0:
  10.3 37.0 all-reduce.5
  51.4 78.1 all-reduce.3
  135.4 31.1 all-reduce.7
where the time goes:
time: 201 us; the launch traced here: 200 us
  waiting for transfers between devices  83.7 us (42%)
  other arithmetic  49.9 us (25%)
  blocking collectives  31.2 us (16%)
  matrix products  20.2 us (10%)
  between operations  13.9 us (7%)
    psum x1, waiting for transfers between devices, body(): lax.psum(jnp.sum(partial_value * factor_c[None, :, :], axis=1), ('ia', 'k...  58.4 us
    psum x1, blocking collectives, body(): lax.psum(jnp.sum(partial_value * factor_b[:, None, :], axis=0), ('ia', 'j...  31.2 us
    psum x1, waiting for transfers between devices, body(): lax.psum(jnp.dot(factor_a.T, factor_a, precision=high, preferred_element_...  25.2 us
    another operation x6, other arithmetic, right_solve(): lower = jnp.linalg.cholesky(system)  24.8 us
    another operation x4, other arithmetic, right_solve(): lax.linalg.triangular_solve(lower, rhs, left_side=False, lower=True, tran...  20.9 us
    dot_general x1, matrix products, body(): jnp.dot(tensor.reshape(mode_two * mode_three, mode_one), factor_a, precis...  12.6 us
  transfers between devices with their start and end apart: 3, of which 2 were waited for; matrix products, arithmetic and copies ran while one was open for 19% of the time, Pallas kernels for 0%

commit v1 on v0

--- a/solution.py
+++ b/solution.py
@@ -27,7 +27,7 @@
         preferred_element_type=jnp.float32,
     )
     partial_value = flat.reshape(mode_two, mode_three, rank)
-    mttkrp_b = lax.psum(jnp.sum(partial_value * factor_c[None, :, :], axis=1), ("ia", "ka"))
+    mttkrp_b = lax.psum(lax.psum(jnp.sum(partial_value * factor_c[None, :, :], axis=1), "ka"), "ia")
     factor_b = right_solve(mttkrp_b, system_b)
     mttkrp_c = lax.psum(jnp.sum(partial_value * factor_b[:, None, :], axis=0), ("ia", "ja"))
     gram_b = lax.psum(

time: 201 us -> 216 us (1.075)
  waiting for transfers between devices: 83.7 us -> 98.1 us
    psum x2, waiting for transfers between devices: 83.6 us -> 98 us  [the longest x1 56.1 us: body(): lax.psum(lax.psum(jnp.sum(partial_value * factor_c[None, :, :], axis=1),...]
  transfers between devices with their start and end apart: 3 -> 3, of which waited for: 2 -> 2; matrix products, arithmetic and copies ran while one was open for 19% -> 2% of each run, Pallas kernels for 0% -> 0%
where the time goes in v1:
time: 216 us; the launch traced here: 215 us
  waiting for transfers between devices  98.1 us (45%)
  other arithmetic  49.9 us (23%)
  blocking collectives  31.9 us (15%)
  matrix products  20.2 us (9%)
  between operations  13.9 us (6%)
    psum x1, waiting for transfers between devices, body(): lax.psum(lax.psum(jnp.sum(partial_value * factor_c[None, :, :], axis=1),...  56.1 us
    psum x1, waiting for transfers between devices, body(): lax.psum(jnp.sum(partial_value * factor_c[None, :, :], axis=1), 'ka')  41.9 us
    psum x1, blocking collectives, body(): lax.psum(jnp.sum(partial_value * factor_b[:, None, :], axis=0), ('ia', 'j...  31.9 us
    another operation x6, other arithmetic, right_solve(): lower = jnp.linalg.cholesky(system)  24.8 us
    another operation x4, other arithmetic, right_solve(): lax.linalg.triangular_solve(lower, rhs, left_side=False, lower=True, tran...  20.9 us
    dot_general x1, matrix products, body(): jnp.dot(tensor.reshape(mode_two * mode_three, mode_one), factor_a, precis...  12.6 us
  transfers between devices with their start and end apart: 3, of which 2 were waited for; matrix products, arithmetic and copies ran while one was open for 2% of the time, Pallas kernels for 0%

profile of v1, /device:TPU:0, one launch (start us, length us, event | category | flops | bytes accessed | tf_op | source)
XLA Modules:
  0.0 215.4 jit_solution(3703378985220969889)
XLA Ops:
  7.2 0.0 copy-start
  7.2 0.0 copy-start.3
  7.2 0.0 all-reduce.5.cloned.1.call-start
  7.2 0.8 copy-done
  8.1 12.6 %multiply_reduce_fusion.1 = (f32[2048,128]{1,0:T(8,128)}, f32[2048,4,128]{2,0,1:T(8,128)}) fusion(f32[4,128]{1,0:T(4,128)} %param.7, f32[256,128]{1,0:T(8,128)S(1)} %copy-done, f32[2048,4,256]{2,1,0:T(4,128)} %param.5), kind=kOutput, calls=%fused_computation.3 | convolution fusion | flops 3223060480 | bytes 13764608 | tf_op jit(solution)/shard_map/dot_general | solution.py:23
  20.7 0.0 all-reduce.5.cloned.1.call-update
  20.7 0.0 all-reduce.9.cloned.1.call-start
  20.8 1.0 fusion.15
  21.8 41.9 %all-reduce.5.cloned.1.call-done = f32[2048,128]{1,0:T(8,128)} async-done(((f32[2048,128]{1,0:T(8,128)}), f32[2048,128]{1,0:T(8,128)}) %all-reduce.5.cloned.1.call-update) | async-done | bytes 1048592 | tf_op jit(solution)/shard_map/psum | solution.py:30
  63.7 0.0 all-reduce.9.cloned.1.call-update
  63.7 0.2 all-reduce.7.cloned.1.call-start
  63.9 0.0 copy-done.3
  64.0 0.1 copy.8
  64.0 56.1 %all-reduce.9.cloned.1.call-done = (f32[2048,128]{1,0:T(8,128)}, f32[128,128]{0,1:T(8,128)}) async-done(((f32[2048,128]{1,0:T(8,128)}, f32[128,128]{0,1:T(8,128)}), (f32[2048,128]{1,0:T(8,128)}, f32[128,128]{0,1:T(8,128)})) %all-reduce.9.cloned.1.call-update) | async-done | bytes 1114128 | tf_op jit(solution)/shard_map/psum | solution.py:30
  120.2 0.8 mul.24
  121.0 0.1 copy.9
  121.1 11.7 %cholesky.44 = f32[128,128]{1,0:T(8,128)S(1)} custom-call(f32[128,128]{1,0:T(8,128)S(1)} %fusion.14), custom_call_target="Cholesky" | custom-call | tf_op jit(solution)/shard_map/jit(cholesky)/cholesky | solution.py:8
  132.9 0.6 compare_reduce_fusion.1
  133.5 0.7 fusion.3
  134.2 9.8 %custom-call.12 = f32[1,128,128]{1,2,0:T(8,128)S(1)} custom-call(f32[1,128,128]{2,1,0:T(8,128)S(1)} %fusion.3), custom_call_target="InvertDiagBlocksLowerTriangular" | custom-call | tf_op jit(solution)/shard_map/triangular_solve | solution.py:9
  144.0 2.2 %fusion.12 = f32[2048,128]{1,0:T(8,128)S(1)} fusion(f32[2048,128]{1,0:T(8,128)} %get-tuple-element.3, f32[1,128,128]{1,2,0:T(8,128)S(1)} %custom-call.12), kind=kOutput, calls=%fused_computation.17 | convolution fusion | flops 402653184 | bytes 2162688 | tf_op jit(solution)/shard_map/triangular_solve | solution.py:9
  146.2 1.0 fusion.10
  147.2 0.0 copy-start.1
  147.2 0.0 copy-start.2
  147.2 2.4 %fusion.16 = f32[128,128]{0,1:T(8,128)} fusion(f32[2048,128]{1,0:T(8,128)S(1)} %fusion.10), kind=kOutput, calls=%fused_computation.28 | convolution fusion | flops 402653184 | bytes 1114112 | tf_op jit(solution)/shard_map/dot_general | solution.py:34
  149.6 0.0 all-reduce.7.cloned.1.call-update
  149.7 2.5 %multiply_reduce_fusion = f32[4,128]{1,0:T(4,128)S(1)} fusion(f32[2048,4,128]{2,0,1:T(8,128)} %get-tuple-element.6, f32[2048,128]{1,0:T(8,128)S(1)} %fusion.10), kind=kLoop, calls=%fused_computation.2 | loop fusion | flops 2096640 | bytes 5244928 | tf_op jit(solution)/shard_map/reduce_sum | solution.py:32
  152.1 31.9 %psum.38 = f32[4,128]{1,0:T(4,128)S(1)} all-reduce(f32[4,128]{1,0:T(4,128)S(1)} %multiply_reduce_fusion), channel_id=1, replica_groups=mesh['ia'=4,'ja'=4,'ka'=2] {'ia','ja'}, use_global_device_ids=true, to_apply=%region_7.9 | all-reduce | flops 512 | bytes 4096 | tf_op jit(solution)/shard_map/psum | solution.py:32
  184.0 0.0 all-reduce.7.cloned.1.call-done
  184.1 0.0 copy-done.2
  184.1 0.8 mul.27
  184.9 0.1 copy.11
  185.0 11.7 %cholesky.55 = f32[128,128]{1,0:T(8,128)S(1)} custom-call(f32[128,128]{1,0:T(8,128)S(1)} %fusion.9), custom_call_target="Cholesky" | custom-call | tf_op jit(solution)/shard_map/jit(cholesky)/cholesky | solution.py:8
  196.8 0.6 compare_reduce_fusion
  197.4 0.7 fusion.4
  198.1 9.8 %custom-call.13 = f32[1,128,128]{1,2,0:T(8,128)S(1)} custom-call(f32[1,128,128]{2,1,0:T(8,128)S(1)} %fusion.4), custom_call_target="InvertDiagBlocksLowerTriangular" | custom-call | tf_op jit(solution)/shard_map/triangular_solve | solution.py:9
  207.9 0.2 fusion.7
  208.1 0.8 fusion.5
  208.9 0.0 copy-done.1
  (4 shorter events, 0.1 us)
Async XLA Ops:
  7.2 0.9 copy-start
  7.2 56.8 %copy-start.3 = (f32[128,128]{1,0:T(8,128)S(1)}, f32[128,128]{1,0:T(8,128)}, u32[]{:S(2)}) copy-start(f32[128,128]{1,0:T(8,128)} %param.8) | copy-start | bytes 196612
  7.2 56.5 %all-reduce.5.cloned.1.call-start = ((), (), s32[]{:S(2)}) async-start(), calls=%async_computation | async-start | bytes 2097152 | tf_op jit(solution)/shard_map/psum | solution.py:30
  20.7 99.5 %all-reduce.9.cloned.1.call-start = ((), (), s32[]{:S(2)}) async-start(), calls=%async_computation.2 | async-start | bytes 2228224 | tf_op jit(solution)/shard_map/psum | solution.py:30
  63.7 120.3 %all-reduce.7.cloned.1.call-start = ((), (), s32[]{:S(2)}) async-start(), calls=%async_computation.1 | async-start | bytes 131072 | tf_op jit(solution)/shard_map/psum | solution.py:33
  147.2 61.7 %copy-start.1 = (f32[2048,128]{1,0:T(8,128)}, f32[2048,128]{1,0:T(8,128)S(1)}, u32[]{:S(2)}) copy-start(f32[2048,128]{1,0:T(8,128)S(1)} %fusion.10) | copy-start | bytes 3145732
  147.2 36.9 %copy-start.2 = (f32[128,128]{0,1:T(8,128)S(1)}, f32[128,128]{0,1:T(8,128)}, u32[]{:S(2)}) copy-start(f32[128,128]{0,1:T(8,128)} %get-tuple-element.4) | copy-start | bytes 196612
Sparse Core Ops, SparseCore 0:
  20.8 42.8 all-reduce.4
  66.1 53.9 all-reduce.8
  149.8 30.8 all-reduce.6
